TPU v7x, 256 devices: a whole 4x4x8 slice. The times are simulated.
256 devices in a mesh: segment: 2 (over core), rows: 32 (over z, x), dp: 4 (over y).
Axes of the slice: x: 4, y: 4, z: 8, core: 2. Of those that a mesh axis runs over, the one named last changes fastest.
Arguments:
- coarse: bfloat16 [8, 100, 384, 256], P(('segment', 'dp'), None, 'rows'), may hold values from -6 to 6
- target: bfloat16 [8, 64, 384, 256], P(('segment', 'dp'), None, 'rows'), may hold values from -6 to 6
- noise: bfloat16 [8, 32, 64, 64, 144], P(('segment', 'dp'), 'rows'), may hold values from -6 to 6
- regions: int32 [8, 32, 32, 4], P(('segment', 'dp')), may hold values from 0 to 244, as said below
- reg_conv: bfloat16 [128, 900], replicated, may hold values from -0.1875 to 0.1875
- reg_out: bfloat16 [64, 128], replicated, may hold values from -0.5 to 0.5
- conv_one: bfloat16 [128, 1152], replicated, may hold values from -0.1875 to 0.1875
- conv_two: bfloat16 [128, 1152], replicated, may hold values from -0.1875 to 0.1875
- out_proj: bfloat16 [64, 128], replicated, may hold values from -0.5 to 0.5
- step_embed: float32 [32, 128], replicated, may hold values from -3 to 3
Outputs:
- mean_field: bfloat16 [8, 64, 384, 256], P(('segment', 'dp'), None, 'rows')
- owner_loss: float32 [8, 32], P(('segment', 'dp'), 'rows')
- grad_conv_one: float32 [128, 1152], replicated
- grad_conv_two: float32 [128, 1152], replicated
- grad_out_proj: float32 [64, 128], replicated
- grad_embed: float32 [32, 128], replicated
Inputs may be any that keep to these rules, and one draw needn't show every extreme that they name: `regions`: for sample s, strip i and entry k: entry 0 is the patch's row offset within strip i (0 on the last strip), entry 1 its first column, at most 244, entry 2 its owner, entry 3 its noise level below 32. Every owner receives 2 * 32, 32 or 16 patches of a sample; for each owner with 64 there is one with 32 and two with 16. No strip lists more than 2 patches for one owner, and some strip lists exactly 2 for one owner.
All inputs are finite; a program needn't handle non-finite values.
Results may differ from a plain program's by a relative error of at most 0.0048.
Values may be sent and summed in bfloat16 or wider, within the bound.
A program may use at most 192 MiB of HBM per device.

v0:
```python
import math
import jax
import jax.numpy as jnp
from jax import lax
from jax.sharding import PartitionSpec as P

PATCH = 12
TAPS = ((-1, -1), (-1, 0), (-1, 1), (0, -1), (0, 0), (0, 1), (1, -1), (1, 0), (1, 1))


def padded_2(cells, sides, width):
    for axis, dim in sides:
        count = lax.axis_size(axis)
        ends = count - 1
        head = lax.slice_in_dim(cells, 0, width, axis=dim)
        tail = lax.slice_in_dim(cells, cells.shape[dim] - width, cells.shape[dim], axis=dim)
        cells = jnp.concatenate(
            [
                lax.ppermute(tail, axis, [(i, (i + 1) % count) for i in range(ends)]),
                cells,
                lax.ppermute(head, axis, [((i + 1) % count, i) for i in range(ends)]),
            ],
            axis=dim,
        )
    return cells


def shifted_2(block, axis, distance):
    devices = range(lax.axis_size(axis))
    route = [(i - distance, i) for i in devices if i - distance in devices]
    return lax.ppermute(block, axis, route)


def shifted(values, row_step, col_step, stride):
    length = values.shape[-1]
    margin = stride + 1
    widths = [(0, 0)] * (values.ndim - 1) + [(margin, margin)]
    padded = jnp.pad(values, widths)
    offset = margin + row_step * stride + col_step
    moved = lax.slice_in_dim(padded, offset, offset + length, axis=values.ndim - 1)
    column = jnp.arange(length, dtype=jnp.int32) % stride + col_step
    inside = (column >= 0) & (column < stride)
    return jnp.where(inside, moved, jnp.zeros((), moved.dtype))


def columns(values, stride):
    return jnp.concatenate(
        [shifted(values, row_step, col_step, stride) for row_step, col_step in TAPS], axis=-2
    )


def fold(gradients, stride):
    width = gradients.shape[-2] // 9
    result = jnp.zeros(gradients.shape[:-2] + (width, gradients.shape[-1]), jnp.float32)
    for position, (row_step, col_step) in enumerate(TAPS):
        piece = gradients[..., position * width : (position + 1) * width, :]
        result = result + shifted(piece, -row_step, -col_step, stride)
    return result


def noise_levels(level_count):
    steps_f = jnp.arange(level_count, dtype=jnp.float32)
    return 0.1 * jnp.exp(steps_f * (math.log(100.0) / (level_count - 1)))


def silu_slope(values):
    gate = jax.nn.sigmoid(values)
    return gate * (1.0 + values * (1.0 - gate))


def product(form, left, right):
    return jnp.einsum(form, left, right, preferred_element_type=jnp.float32)


def regress(grid_rows, reg_conv, reg_out):
    channels, height, width = grid_rows.shape
    flat = grid_rows.reshape(channels, height * width)
    hidden = product("ok,kp->op", reg_conv, columns(flat, width))
    activated = jax.nn.silu(hidden).astype(jnp.bfloat16)
    mean_flat = product("co,op->cp", reg_out, activated).astype(jnp.bfloat16)
    return mean_flat.reshape(reg_out.shape[0], height, width)


def patch_block(mean_part, target_part, noise_part, step_ids, in_use, weights):
    conv_one, conv_two, out_proj, step_embed = weights
    stride = PATCH
    level_count = step_embed.shape[0]
    sigma_table = noise_levels(level_count)
    step_hot = (step_ids[:, None] == jnp.arange(level_count, dtype=jnp.int32)[None, :]).astype(
        jnp.float32
    )
    sigma = jnp.sum(step_hot * sigma_table[None, :], axis=1)
    sigma_sq = sigma * sigma + 1.0
    scale_in = (1.0 / jnp.sqrt(sigma_sq))[:, None, None]
    scale_skip = (1.0 / sigma_sq)[:, None, None]
    scale_out = (sigma / jnp.sqrt(sigma_sq))[:, None, None]
    weight_loss = sigma_sq / (sigma * sigma)
    mean_float = mean_part.astype(jnp.float32)
    residual = target_part.astype(jnp.float32) - mean_float
    noisy = residual + sigma[:, None, None] * noise_part.astype(jnp.float32)
    inputs = jnp.concatenate([scale_in * noisy, mean_float], axis=1).astype(jnp.bfloat16)
    cols_in = columns(inputs, stride)
    embedded = jnp.sum(step_hot[:, :, None] * step_embed[None, :, :], axis=1)
    pre_one = product("ok,bkp->bop", conv_one, cols_in) + embedded[:, :, None]
    act_one = jax.nn.silu(pre_one).astype(jnp.bfloat16)
    cols_one = columns(act_one, stride)
    pre_two = product("ok,bkp->bop", conv_two, cols_one)
    act_two = jax.nn.silu(pre_two).astype(jnp.bfloat16)
    output = product("co,bop->bcp", out_proj, act_two)
    error = scale_skip * noisy + scale_out * output - residual
    losses = weight_loss * jnp.mean(error * error, axis=(1, 2)) * in_use
    factor = 2.0 * weight_loss * in_use / (error.shape[1] * error.shape[2])
    grad_output = (factor[:, None, None] * scale_out * error).astype(jnp.bfloat16)
    grad_proj = product("bcp,bop->co", grad_output, act_two)
    grad_act_two = product("co,bcp->bop", out_proj, grad_output)
    grad_pre_two = (grad_act_two * silu_slope(pre_two)).astype(jnp.bfloat16)
    grad_two = product("bop,bkp->ok", grad_pre_two, cols_one)
    grad_cols = product("ok,bop->bkp", conv_two, grad_pre_two)
    grad_act_one = fold(grad_cols, stride)
    grad_pre_one = (grad_act_one * silu_slope(pre_one)).astype(jnp.bfloat16)
    grad_one = product("bop,bkp->ok", grad_pre_one, cols_in)
    pixel_sums = jnp.sum(grad_pre_one, axis=2, dtype=jnp.float32)
    grad_table = jnp.sum(step_hot[:, :, None] * pixel_sums[:, None, :], axis=0)
    return (losses, (grad_one, grad_two, grad_proj, grad_table))


def run_blocks(mean_part, target_part, noise_part, step_ids, in_use, weights):
    patch_count = mean_part.shape[0]
    blocks = patch_count // 4

    def regroup(values):
        return values.reshape((blocks, 4) + values.shape[1:])

    def advance(running, group_block):
        losses, gradients = patch_block(
            group_block[0], group_block[1], group_block[2], group_block[3], group_block[4], weights
        )
        summed = (
            running[0] + gradients[0],
            running[1] + gradients[1],
            running[2] + gradients[2],
            running[3] + gradients[3],
        )
        return (summed, losses)

    initial = (
        jnp.zeros(weights[0].shape, jnp.float32),
        jnp.zeros(weights[1].shape, jnp.float32),
        jnp.zeros(weights[2].shape, jnp.float32),
        jnp.zeros(weights[3].shape, jnp.float32),
    )
    stacked = (
        regroup(mean_part),
        regroup(target_part),
        regroup(noise_part),
        regroup(step_ids),
        regroup(in_use),
    )
    gradients, losses = lax.scan(advance, initial, stacked)
    return (losses.reshape(patch_count), gradients)


def owner_tables(region_rows, strips):
    owners = region_rows[:, :, 2]
    owner_hot = (owners[:, :, None] == jnp.arange(strips, dtype=jnp.int32)[None, None, :]).astype(
        jnp.int32
    )
    pair_rank = jnp.sum((jnp.cumsum(owner_hot, axis=1) - owner_hot) * owner_hot, axis=2)
    flat_hot = owner_hot.reshape(-1, strips)
    owner_slot = jnp.sum((jnp.cumsum(flat_hot, axis=0) - flat_hot) * flat_hot, axis=1).reshape(
        owners.shape
    )
    return (owners, pair_rank, owner_slot)


def owned_slots(region_rows, owners, pair_rank, owner_slot, strip_index, capacity, most, height):
    strips = region_rows.shape[0]
    slot_hits = (
        (owners == strip_index)[:, :, None]
        & (owner_slot[:, :, None] == jnp.arange(most, dtype=jnp.int32)[None, None, :])
    ).astype(jnp.int32)
    strip_ids = jnp.arange(strips, dtype=jnp.int32)[:, None]
    recv_index = jnp.sum(slot_hits * (strip_ids * capacity + pair_rank)[:, :, None], axis=(0, 1))
    in_use = jnp.sum(slot_hits, axis=(0, 1)).astype(jnp.float32)
    step_ids = jnp.sum(slot_hits * region_rows[:, :, 3][:, :, None], axis=(0, 1))
    row_at = jnp.sum(
        slot_hits * (strip_ids * height + region_rows[:, :, 0])[:, :, None], axis=(0, 1)
    )
    col_at = jnp.sum(slot_hits * region_rows[:, :, 1][:, :, None], axis=(0, 1))
    return (recv_index, in_use, step_ids, row_at, col_at)


def cut_patches(source_grid, row_at, col_at, height):
    zero_index = jnp.zeros((), jnp.int32)

    def cut(row_start, col_start):
        piece = lax.dynamic_slice(
            source_grid,
            (zero_index, zero_index, row_start, col_start),
            (2, source_grid.shape[1], height, height),
        )
        return piece.reshape(2, source_grid.shape[1], height * height)

    return jax.vmap(cut)(row_at, col_at)


def per_device(
    coarse, target, noise, regions, reg_conv, reg_out, conv_one, conv_two, out_proj, step_embed
):
    strips = lax.axis_size("rows")
    strip_index = lax.axis_index("rows")
    region_rows = regions[0]
    per_strip = region_rows.shape[1]
    capacity = max(2, (2 * per_strip + strips - 1) // strips)
    most = 2 * per_strip
    weights = (conv_one, conv_two, out_proj, step_embed)
    rimmed = padded_2(coarse, (("rows", 2),), 1)
    mean_strip = regress(rimmed[0], reg_conv, reg_out)[:, 1:-1]
    height = mean_strip.shape[1]
    pair_strip = jnp.stack([mean_strip, target[0]])
    owners, pair_rank, owner_slot = owner_tables(region_rows, strips)
    own_regions = lax.dynamic_index_in_dim(region_rows, strip_index, 0, keepdims=False)
    own_pairs = lax.dynamic_index_in_dim(pair_rank, strip_index, 0, keepdims=False)
    slot_noise = noise[0, 0]
    below = shifted_2(pair_strip[:, :, : height - 1], "rows", -1)
    extended = jnp.concatenate([pair_strip, below], axis=2)
    patches = cut_patches(extended, own_regions[:, 0], own_regions[:, 1], height)
    outgoing = jnp.zeros((strips, capacity) + patches.shape[1:], patches.dtype)
    outgoing = outgoing.at[own_regions[:, 2], own_pairs].set(patches)
    received = lax.all_to_all(outgoing, "rows", split_axis=0, concat_axis=0, tiled=True)
    flat_recv = received.reshape((strips * capacity,) + patches.shape[1:])
    recv_index, in_use, step_ids, row_at, col_at = owned_slots(
        region_rows, owners, pair_rank, owner_slot, strip_index, capacity, most, height
    )
    gathered = jnp.take(flat_recv, recv_index, axis=0)
    losses, gradients = run_blocks(
        gathered[:, 0], gathered[:, 1], slot_noise, step_ids, in_use, weights
    )
    owner_total = jnp.sum(losses)
    totals = lax.psum(
        (gradients[0], gradients[1], gradients[2], gradients[3]), ("segment", "rows", "dp")
    )
    return (mean_strip[None], owner_total.reshape(1, 1), totals[0], totals[1], totals[2], totals[3])


def solution(mesh):
    placed = (
        P(("segment", "dp"), None, "rows", None),
        P(("segment", "dp"), None, "rows", None),
        P(("segment", "dp"), "rows", None, None, None),
        P(("segment", "dp"), None, None, None),
        P(),
        P(),
        P(),
        P(),
        P(),
        P(),
    )
    return jax.shard_map(
        per_device,
        mesh=mesh,
        in_specs=placed,
        out_specs=(
            P(("segment", "dp"), None, "rows", None),
            P(("segment", "dp"), "rows"),
            P(),
            P(),
            P(),
            P(),
        ),
        check_vma=False,
    )
```

profile of v0, /device:TPU:8, one launch (start us, length us, event | category | flops | bytes accessed | tf_op | source)
XLA Modules:
  0.0 851.5 jit_solution(5382771631686754666)
XLA Ops:
  8.1 3.4 collective-permute-start
  12.8 3.2 copy.114
  18.2 4.4 slice_select_fusion.1
  22.6 41.7 %concatenate.38 = bf16[900,3584]{1,0:T(8,128)(2,1)} concatenate(bf16[100,3584]{1,0:T(8,128)(2,1)} %get-tuple-element.387, bf16[100,3584]{1,0:T(8,128)(2,1)} %get-tuple-element.390, bf16[100,3584]{1,0:T(8,128)(2,1)} %get-tuple-element.380, bf16[100,3584]{1,0:T(8,128)(2,1)} %get-tuple-element.388, bf16[100,3584]{1,0:T(8,128)(2,1)} %get-tuple-element.391, ...), dimensions={0} | concatenate | bytes 12902400 | tf_op jit(solution)/shard_map/concatenate | solution.py:47
  64.3 5.4 fusion.29
  71.2 3.2 copy.113
  74.4 4.9 pad_maximum_fusion.2
  79.3 4.6 copy.115
  87.4 16.4 %collective-permute-done.2 = bf16[2,64,11,256]{3,1,2,0:T(8,128)(2,1)} collective-permute-done((bf16[2,64,11,256]{3,1,2,0:T(8,128)(2,1)}, bf16[2,64,11,256]{3,1,2,0:T(8,128)(2,1)}, u32[]{:S(2)}, u32[]{:S(2)}) %collective-permute-start.2) | collective-permute-done | bytes 720928 | tf_op jit(solution)/shard_map/ppermute | solution.py:31
  103.8 4.7 copy.116
  108.4 8.1 pad_maximum_fusion.1
  116.5 8.6 %gather_fusion = bf16[32,2,64,12,12]{2,1,4,3,0:T(2,128)(2,1)S(1)} fusion(bf16[2,64,23,256]{1,0,3,2:T(2,128)(2,1)} %pad_maximum_fusion.1, s32[32]{0:T(128)S(1)} %get-tuple-element.398), kind=kCustom, calls=%fused_computation | custom fusion | bytes 2359808 | tf_op jit(solution)/shard_map/vmap()/gather | solution.py:197
  125.2 3.9 copy.117
  129.1 2.5 broadcast_in_dim.229
  131.6 5.7 scatter_fusion
  137.3 15.6 %all-to-all-start = ((bf16[32,2,2,64,144]{4,3,2,1,0:T(8,128)(2,1)}), bf16[32,2,2,64,144]{4,3,2,1,0:T(8,128)(2,1)}, u32[]{:S(2)}, u32[]{:S(2)}) async-start(bf16[32,2,2,64,144]{4,3,2,1,0:T(8,128)(2,1)} %scatter_fusion), calls=%async_computation | async-start | bytes 8388608 | tf_op jit(solution)/shard_map/all_to_all | solution.py:230
  153.4 9.0 %reduce-window.6 = s32[32,8,128]{2,1,0:T(8,128)S(1)} reduce-window(s32[32,8,128]{2,1,0:T(8,128)S(1)} %fusion.38, s32[]{:T(128)} %constant.269.clone.1), window={size=1x1x128 pad=0_0x0_0x127_0}, to_apply=%region_0.1 | reduce-window | flops 4161536 | bytes 262148 | tf_op jit(solution)/shard_map/reduce-window
  164.0 81.0 %all-to-all-done = bf16[32,2,2,64,144]{4,3,2,1,0:T(8,128)(2,1)} async-done(((bf16[32,2,2,64,144]{4,3,2,1,0:T(8,128)(2,1)}), bf16[32,2,2,64,144]{4,3,2,1,0:T(8,128)(2,1)}, u32[]{:S(2)}, u32[]{:S(2)}) %all-to-all-start) | async-done | bytes 2359328 | tf_op jit(solution)/shard_map/all_to_all | solution.py:230
  245.0 5.0 gather_fusion.1
  250.0 2.6 broadcast_select_fusion
  252.6 2.5 fusion.65
  255.2 328.0 %while.21 = (s32[]{:T(128)}, f32[128,1152]{1,0:T(8,128)}, f32[128,1152]{1,0:T(8,128)}, f32[64,128]{1,0:T(8,128)S(1)}, f32[32,128]{1,0:T(8,128)S(1)}, /*index=5*/...) while((s32[]{:T(128)}, f32[128,1152]{1,0:T(8,128)}, ...), condition=%wide.region_15.16_spmd.clone, body=%wide.region_9.15_spmd.clone.sunk | while | flops 884677568 | bytes 48410204 | solution.py:159
  259.0 2.3 multiply_convert_fusion.15
  262.6 1.6 multiply_convert_fusion.16
  267.4 1.7 fusion.117
  278.5 2.3 multiply_convert_fusion.15
  282.2 1.6 multiply_convert_fusion.16
  286.9 2.8 fusion.117
  299.1 2.3 multiply_convert_fusion.15
  302.7 1.6 multiply_convert_fusion.16
  307.5 2.8 fusion.117
  319.6 2.3 multiply_convert_fusion.15
  323.3 1.6 multiply_convert_fusion.16
  328.0 2.8 fusion.117
  340.2 2.3 multiply_convert_fusion.15
  348.6 2.8 fusion.117
  360.8 2.3 multiply_convert_fusion.15
  369.2 2.8 fusion.117
  381.3 2.3 multiply_convert_fusion.15
  389.7 2.8 fusion.117
  401.9 2.3 multiply_convert_fusion.15
  410.3 2.8 fusion.117
  422.5 2.3 multiply_convert_fusion.15
  430.9 2.8 fusion.117
  443.0 2.3 multiply_convert_fusion.15
  451.4 2.8 fusion.117
  463.6 2.3 multiply_convert_fusion.15
  472.0 2.8 fusion.117
  484.2 2.3 multiply_convert_fusion.15
  492.5 2.8 fusion.117
  504.7 2.3 multiply_convert_fusion.15
  513.1 2.8 fusion.117
  525.3 2.3 multiply_convert_fusion.15
  528.9 1.6 multiply_convert_fusion.16
  533.7 2.8 fusion.117
  545.9 2.3 multiply_convert_fusion.15
  549.5 1.6 multiply_convert_fusion.16
  554.2 2.8 fusion.117
  566.4 2.3 multiply_convert_fusion.15
  574.8 2.8 fusion.117
  584.5 74.9 %all-reduce.11 = (f32[64,128]{1,0:T(8,128)}, f32[32,128]{1,0:T(8,128)}) all-reduce(f32[64,128]{1,0:T(8,128)S(1)} %get-tuple-element.201, f32[32,128]{1,0:T(8,128)S(1)} %get-tuple-element.202), channel_id=1, replica_groups=mesh['segment'=2,'rows'=32,'dp'=4] {'segment','rows','dp'}, use_global_device_ids=true, to_apply=%region_19.20 | all-reduce | flops 12288 | bytes 98304 | tf_op jit(solution)/shard_map/psum | solution.py:240
  659.4 181.4 %all-reduce.15.cloned.1.call-done = (f32[128,1152]{1,0:T(8,128)}, f32[128,1152]{1,0:T(8,128)}) async-done(((f32[128,1152]{1,0:T(8,128)}, f32[128,1152]{1,0:T(8,128)}), (f32[128,1152]{1,0:T(8,128)}, f32[128,1152]{1,0:T(8,128)})) %all-reduce.15.cloned.1.call-update) | async-done | bytes 1179664 | tf_op jit(solution)/shard_map/psum | solution.py:240
  840.8 1.9 copy.178
  842.7 1.9 copy.179
  (877 shorter events, 245.5 us)
Async XLA Ops:
  7.2 57.2 %copy-start = (bf16[128,900]{0,1:T(8,128)(2,1)S(1)}, bf16[128,900]{0,1:T(8,128)(2,1)}, u32[]{:S(2)}) copy-start(bf16[128,900]{0,1:T(8,128)(2,1)} %param.16) | copy-start | bytes 691204
  7.2 10.4 %copy-start.9 = (bf16[1,100,12,256]{3,1,2,0:T(8,128)(2,1)S(1)}, bf16[1,100,12,256]{3,1,2,0:T(8,128)(2,1)}, u32[]{:S(2)}) copy-start(bf16[1,100,12,256]{3,1,2,0:T(8,128)(2,1)} %param.12) | copy-start | bytes 1843204
  8.1 8.8 %collective-permute-start = (bf16[1,100,1,256]{3,1,2,0:T(8,128)(2,1)S(1)}, bf16[1,100,1,256]{3,1,2,0:T(8,128)(2,1)S(1)}, u32[]{:S(2)}, u32[]{:S(2)}) collective-permute-start(bf16[1,100,1,256]{3,1,2,0:T(8,128)(2,1)S(1)} %get-tuple-element.393), channel_id=1, source_target_pairs={{0,4},{4,8},{8,12},{12,16},{16,20},{20,24},{24,28},{28,32},{32,36}... | collective-permute-start | bytes 153608 | tf_op jit(solution)/shard_map/ppermute | solution.py:19
  11.5 6.0 collective-permute-start.1
  22.6 41.7 %copy-start.12 = (bf16[64,128]{1,0:T(8,128)(2,1)S(1)}, bf16[64,128]{1,0:T(8,128)(2,1)}, u32[]{:S(2)}) copy-start(bf16[64,128]{1,0:T(8,128)(2,1)} %param.17) | copy-start | bytes 49156
  83.9 19.9 %collective-permute-start.2 = (bf16[2,64,11,256]{3,1,2,0:T(8,128)(2,1)}, bf16[2,64,11,256]{3,1,2,0:T(8,128)(2,1)}, u32[]{:S(2)}, u32[]{:S(2)}) collective-permute-start(bf16[2,64,11,256]{3,1,2,0:T(8,128)(2,1)} %copy.115), channel_id=1, source_target_pairs={{4,0},{8,4},{12,8},{16,12},{20,16},{24,20},{28,24},{32,28},{36,32}... | collective-permute-start | bytes 2162696 | tf_op jit(solution)/shard_map/ppermute | solution.py:31
  129.1 2.5 copy-start.7
  137.3 107.7 %all-to-all-start = ((bf16[32,2,2,64,144]{4,3,2,1,0:T(8,128)(2,1)}), bf16[32,2,2,64,144]{4,3,2,1,0:T(8,128)(2,1)}, u32[]{:S(2)}, u32[]{:S(2)}) async-start(bf16[32,2,2,64,144]{4,3,2,1,0:T(8,128)(2,1)} %scatter_fusion), calls=%async_computation | async-start | bytes 8388608 | tf_op jit(solution)/shard_map/all_to_all | solution.py:230
  152.9 687.9 %all-reduce.15.cloned.1.call-start = ((), (), s32[]{:S(2)}) async-start(), calls=%async_computation.1 | async-start | bytes 2359296 | tf_op jit(solution)/shard_map/psum | solution.py:240
  252.6 2.6 copy-start.8
  252.6 2.6 copy-start.10
  252.6 2.6 copy-start.11
  262.6 2.9 copy-start.2
  265.6 1.8 copy-start.3
  271.0 1.3 copy-start.4
  273.2 1.5 copy-start.5
  282.1 2.9 copy-start.2
  285.1 1.8 copy-start.3
  291.6 1.3 copy-start.4
  293.8 1.5 copy-start.5
  302.7 2.9 copy-start.2
  305.6 1.8 copy-start.3
  312.1 1.3 copy-start.4
  314.3 1.5 copy-start.5
  323.3 2.9 copy-start.2
  326.2 1.8 copy-start.3
  334.9 1.5 copy-start.5
  343.8 2.9 copy-start.2
  346.8 1.8 copy-start.3
  355.5 1.5 copy-start.5
  364.4 2.9 copy-start.2
  367.3 1.8 copy-start.3
  376.0 1.5 copy-start.5
  385.0 2.9 copy-start.2
  387.9 1.8 copy-start.3
  396.6 1.5 copy-start.5
  405.5 2.9 copy-start.2
  408.5 1.8 copy-start.3
  417.2 1.5 copy-start.5
  426.1 2.9 copy-start.2
  429.0 1.8 copy-start.3
  437.7 1.5 copy-start.5
  446.6 2.9 copy-start.2
  449.6 1.8 copy-start.3
  458.3 1.5 copy-start.5
  467.2 2.9 copy-start.2
  470.2 1.8 copy-start.3
  478.9 1.5 copy-start.5
  487.8 2.9 copy-start.2
  490.7 1.8 copy-start.3
  499.4 1.5 copy-start.5
  508.3 2.9 copy-start.2
  511.3 1.8 copy-start.3
  520.0 1.5 copy-start.5
  528.9 2.9 copy-start.2
  531.9 1.8 copy-start.3
  540.6 1.5 copy-start.5
  549.5 2.9 copy-start.2
  552.4 1.8 copy-start.3
  561.1 1.5 copy-start.5
  570.0 2.9 copy-start.2
  573.0 1.8 copy-start.3
  581.7 1.5 copy-start.5
  583.2 261.5 %copy-start.1 = (bf16[128,900]{0,1:T(8,128)(2,1)S(1)}, bf16[128,900]{0,1:T(8,128)(2,1)}, u32[]{:S(2)}) copy-start(bf16[128,900]{0,1:T(8,128)(2,1)} %param.16) | copy-start | bytes 691204
  (29 other events, 33.2 us)
Sparse Core Ops, SparseCore 0:
  583.3 257.4 all-reduce.14
where the time goes:
time: 859 us; the launch traced here: 851 us
  waiting for transfers between devices  279 us (32%)
  matrix products  190 us (22%)
  local copies, waits for them, and re-layouts  148 us (17%)
  other arithmetic  119 us (14%)
  blocking collectives  74.9 us (9%)
  starting transfers between devices  22 us (3%)
  between operations  14.3 us (2%)
    dot_general x129, matrix products, product(): return jnp.einsum(form, left, right, preferred_element_type=jnp.float32)  190 us
    psum x1, waiting for transfers between devices, per_device(): lax.psum((gradients[0], gradients[1], gradients[2], gradients[3]), ('segm...  181 us
    all_to_all x1, waiting for transfers between devices, per_device(): lax.all_to_all(outgoing, 'rows', split_axis=0, concat_axis=0, tiled=True)  81 us
    psum x1, blocking collectives, per_device(): lax.psum((gradients[0], gradients[1], gradients[2], gradients[3]), ('segm...  74.9 us
    concatenate x1, local copies, waits for them, and re-layouts, columns(): jnp.concatenate([shifted(values, row_step, col_step, stride) for row_step...  41.7 us
    while x256, other arithmetic  34.1 us
    another operation x19, other arithmetic  27.5 us
    dynamic_update_slice x16, local copies, waits for them, and re-layouts, run_blocks(): gradients, losses = lax.scan(advance, initial, stacked)  21.3 us
  transfers between devices with their start and end apart: 5, of which 4 were waited for; matrix products, arithmetic and copies ran while one was open for 2% of the time, Pallas kernels for 0%

commit v1 on v0

--- a/solution.py
+++ b/solution.py
@@ -237,9 +237,9 @@
         gathered[:, 0], gathered[:, 1], slot_noise, step_ids, in_use, weights
     )
     owner_total = jnp.sum(losses)
-    totals = lax.psum(
-        (gradients[0], gradients[1], gradients[2], gradients[3]), ("segment", "rows", "dp")
-    )
+    totals = (gradients[0], gradients[1], gradients[2], gradients[3])
+    for dev in ("segment", ("rows", "dp")):
+        totals = lax.psum(totals, dev)
     return (mean_strip[None], owner_total.reshape(1, 1), totals[0], totals[1], totals[2], totals[3])
 
 

time: 859 us -> 1310 us (1.53)
  blocking collectives: 74.9 us -> 686 us
  waiting for transfers between devices: 279 us -> 127 us
    psum x1 -> x2, blocking collectives: 74.9 us -> 686 us  [per_device(): totals = lax.psum(totals, dev)]
    psum x1 -> x2, waiting for transfers between devices: 181 us -> 29.2 us  [per_device(): totals = lax.psum(totals, dev)]
    dynamic_update_slice x16, local copies, waits for them, and re-layouts: 21.3 us -> 0.61 us  [run_blocks(): gradients, losses = lax.scan(advance, initial, stacked)]
  transfers between devices with their start and end apart: 5 -> 6, of which waited for: 4 -> 4; matrix products, arithmetic and copies ran while one was open for 2% -> 1% of each run, Pallas kernels for 0% -> 0%
where the time goes in v1:
time: 1310 us; the launch traced here: 1300 us
  blocking collectives  686 us (52%)
  matrix products  190 us (15%)
  local copies, waits for them, and re-layouts  138 us (11%)
  waiting for transfers between devices  127 us (10%)
  other arithmetic  118 us (9%)
  starting transfers between devices  22 us (2%)
  between operations  14.3 us (1%)
    psum x2, blocking collectives, per_device(): totals = lax.psum(totals, dev)  686 us
    dot_general x129, matrix products, product(): return jnp.einsum(form, left, right, preferred_element_type=jnp.float32)  190 us
    all_to_all x1, waiting for transfers between devices, per_device(): lax.all_to_all(outgoing, 'rows', split_axis=0, concat_axis=0, tiled=True)  81 us
    concatenate x1, local copies, waits for them, and re-layouts, columns(): jnp.concatenate([shifted(values, row_step, col_step, stride) for row_step...  41.7 us
    while x256, other arithmetic  34.1 us
    psum x2, waiting for transfers between devices, per_device(): totals = lax.psum(totals, dev)  29.2 us
    another operation x19, other arithmetic  27.5 us
  transfers between devices with their start and end apart: 6, of which 4 were waited for; matrix products, arithmetic and copies ran while one was open for 1% of the time, Pallas kernels for 0%

profile of v1, /device:TPU:8, one launch (start us, length us, event | category | flops | bytes accessed | tf_op | source)
XLA Modules:
  0.0 1299.1 jit_solution(337058999632106801)
XLA Ops:
  8.1 3.4 collective-permute-start
  12.8 3.2 copy.114
  18.2 4.4 slice_select_fusion.1
  22.6 41.7 %concatenate.38 = bf16[900,3584]{1,0:T(8,128)(2,1)} concatenate(bf16[100,3584]{1,0:T(8,128)(2,1)} %get-tuple-element.391, bf16[100,3584]{1,0:T(8,128)(2,1)} %get-tuple-element.394, bf16[100,3584]{1,0:T(8,128)(2,1)} %get-tuple-element.384, bf16[100,3584]{1,0:T(8,128)(2,1)} %get-tuple-element.392, bf16[100,3584]{1,0:T(8,128)(2,1)} %get-tuple-element.395, ...), dimensions={0} | concatenate | bytes 12902400 | tf_op jit(solution)/shard_map/concatenate | solution.py:47
  64.3 5.4 fusion.29
  71.2 3.2 copy.113
  74.4 4.9 pad_maximum_fusion.2
  79.3 4.6 copy.115
  87.4 16.4 %collective-permute-done.2 = bf16[2,64,11,256]{3,1,2,0:T(8,128)(2,1)} collective-permute-done((bf16[2,64,11,256]{3,1,2,0:T(8,128)(2,1)}, bf16[2,64,11,256]{3,1,2,0:T(8,128)(2,1)}, u32[]{:S(2)}, u32[]{:S(2)}) %collective-permute-start.2) | collective-permute-done | bytes 720928 | tf_op jit(solution)/shard_map/ppermute | solution.py:31
  103.8 4.7 copy.116
  108.4 8.1 pad_maximum_fusion.1
  116.5 8.6 gather_fusion
  125.2 3.9 copy.117
  129.1 2.5 broadcast_in_dim.229
  131.6 5.7 scatter_fusion
  137.3 15.6 %all-to-all-start = ((bf16[32,2,2,64,144]{4,3,2,1,0:T(8,128)(2,1)}), bf16[32,2,2,64,144]{4,3,2,1,0:T(8,128)(2,1)}, u32[]{:S(2)}, u32[]{:S(2)}) async-start(bf16[32,2,2,64,144]{4,3,2,1,0:T(8,128)(2,1)} %scatter_fusion), calls=%async_computation | async-start | bytes 8388608 | tf_op jit(solution)/shard_map/all_to_all | solution.py:230
  153.4 9.0 reduce-window.6
  164.0 81.0 %all-to-all-done = bf16[32,2,2,64,144]{4,3,2,1,0:T(8,128)(2,1)} async-done(((bf16[32,2,2,64,144]{4,3,2,1,0:T(8,128)(2,1)}), bf16[32,2,2,64,144]{4,3,2,1,0:T(8,128)(2,1)}, u32[]{:S(2)}, u32[]{:S(2)}) %all-to-all-start) | async-done | bytes 2359328 | tf_op jit(solution)/shard_map/all_to_all | solution.py:230
  245.0 5.0 gather_fusion.1
  250.0 2.6 broadcast_select_fusion
  252.6 2.5 fusion.65
  255.2 317.5 %while.21 = (s32[]{:T(128)}, f32[128,1152]{1,0:T(8,128)}, f32[128,1152]{1,0:T(8,128)}, f32[64,128]{1,0:T(8,128)S(1)}, f32[32,128]{1,0:T(8,128)S(1)}, /*index=5*/...) while((s32[]{:T(128)}, f32[128,1152]{1,0:T(8,128)}, ...), condition=%wide.region_15.16_spmd.clone, body=%wide.region_9.15_spmd.clone.sunk | while | flops 884677568 | bytes 48410204 | solution.py:159
  259.0 2.3 multiply_convert_fusion.15
  262.6 1.6 multiply_convert_fusion.16
  267.4 1.7 fusion.117
  277.9 2.3 multiply_convert_fusion.15
  281.5 1.6 multiply_convert_fusion.16
  286.3 2.8 fusion.117
  297.8 2.3 multiply_convert_fusion.15
  306.2 2.8 fusion.117
  317.7 2.3 multiply_convert_fusion.15
  326.1 2.8 fusion.117
  337.6 2.3 multiply_convert_fusion.15
  346.0 2.8 fusion.117
  357.5 2.3 multiply_convert_fusion.15
  361.1 1.6 multiply_convert_fusion.16
  365.9 2.8 fusion.117
  377.4 2.3 multiply_convert_fusion.15
  385.8 2.8 fusion.117
  397.3 2.3 multiply_convert_fusion.15
  405.7 2.8 fusion.117
  417.2 2.3 multiply_convert_fusion.15
  425.6 2.8 fusion.117
  437.1 2.3 multiply_convert_fusion.15
  445.5 2.8 fusion.117
  457.0 2.3 multiply_convert_fusion.15
  460.7 1.6 multiply_convert_fusion.16
  465.4 2.8 fusion.117
  476.9 2.3 multiply_convert_fusion.15
  485.3 2.8 fusion.117
  496.8 2.3 multiply_convert_fusion.15
  500.5 1.6 multiply_convert_fusion.16
  505.2 2.8 fusion.117
  516.8 2.3 multiply_convert_fusion.15
  525.1 2.8 fusion.117
  536.7 2.3 multiply_convert_fusion.15
  545.0 2.8 fusion.117
  556.6 2.3 multiply_convert_fusion.15
  565.0 2.8 fusion.117
  572.7 29.2 %all-reduce.20.cloned.1.call-done = (f32[128,1152]{1,0:T(8,128)}, f32[128,1152]{1,0:T(8,128)}) async-done(((f32[128,1152]{1,0:T(8,128)}, f32[128,1152]{1,0:T(8,128)}), (f32[128,1152]{1,0:T(8,128)}, f32[128,1152]{1,0:T(8,128)})) %all-reduce.20.cloned.1.call-update) | async-done | bytes 1179664 | tf_op jit(solution)/shard_map/psum | solution.py:242
  602.6 3.6 all-reduce.13
  606.2 682.2 %all-reduce.11 = (f32[64,128]{1,0:T(8,128)}, f32[32,128]{1,0:T(8,128)}) all-reduce(f32[64,128]{1,0:T(8,128)S(1)} %get-tuple-element.354, f32[32,128]{1,0:T(8,128)S(1)} %get-tuple-element.355), channel_id=1, replica_groups=mesh['segment'=2,'rows'=32,'dp'=4] {'rows','dp'}, use_global_device_ids=true, to_apply=%region_22.23 | all-reduce | flops 12288 | bytes 98304 | tf_op jit(solution)/shard_map/psum | solution.py:242
  1288.5 1.9 copy.180
  1290.4 1.9 copy.181
  (881 shorter events, 235.9 us)
Async XLA Ops:
  7.2 57.2 %copy-start = (bf16[128,900]{0,1:T(8,128)(2,1)S(1)}, bf16[128,900]{0,1:T(8,128)(2,1)}, u32[]{:S(2)}) copy-start(bf16[128,900]{0,1:T(8,128)(2,1)} %param.16) | copy-start | bytes 691204
  7.2 10.4 copy-start.9
  8.1 8.8 collective-permute-start
  11.5 6.0 collective-permute-start.1
  22.6 41.7 %copy-start.12 = (bf16[64,128]{1,0:T(8,128)(2,1)S(1)}, bf16[64,128]{1,0:T(8,128)(2,1)}, u32[]{:S(2)}) copy-start(bf16[64,128]{1,0:T(8,128)(2,1)} %param.17) | copy-start | bytes 49156
  83.9 19.9 %collective-permute-start.2 = (bf16[2,64,11,256]{3,1,2,0:T(8,128)(2,1)}, bf16[2,64,11,256]{3,1,2,0:T(8,128)(2,1)}, u32[]{:S(2)}, u32[]{:S(2)}) collective-permute-start(bf16[2,64,11,256]{3,1,2,0:T(8,128)(2,1)} %copy.115), channel_id=1, source_target_pairs={{4,0},{8,4},{12,8},{16,12},{20,16},{24,20},{28,24},{32,28},{36,32}... | collective-permute-start | bytes 2162696 | tf_op jit(solution)/shard_map/ppermute | solution.py:31
  129.1 2.5 copy-start.7
  137.3 107.7 %all-to-all-start = ((bf16[32,2,2,64,144]{4,3,2,1,0:T(8,128)(2,1)}), bf16[32,2,2,64,144]{4,3,2,1,0:T(8,128)(2,1)}, u32[]{:S(2)}, u32[]{:S(2)}) async-start(bf16[32,2,2,64,144]{4,3,2,1,0:T(8,128)(2,1)} %scatter_fusion), calls=%async_computation | async-start | bytes 8388608 | tf_op jit(solution)/shard_map/all_to_all | solution.py:230
  152.9 449.0 %all-reduce.20.cloned.1.call-start = ((), (), s32[]{:S(2)}) async-start(), calls=%async_computation.2 | async-start | bytes 2359296 | tf_op jit(solution)/shard_map/psum | solution.py:242
  252.6 2.6 copy-start.8
  252.6 2.6 copy-start.10
  252.6 2.6 copy-start.11
  262.6 2.9 copy-start.2
  265.6 1.8 copy-start.3
  269.9 1.0 copy-start.6
  271.0 1.3 copy-start.4
  281.5 2.9 copy-start.2
  284.4 1.8 copy-start.3
  290.9 1.3 copy-start.4
  301.4 2.9 copy-start.2
  304.3 1.8 copy-start.3
  309.8 1.0 copy-start.6
  310.8 1.3 copy-start.4
  321.3 2.9 copy-start.2
  324.2 1.8 copy-start.3
  330.7 1.3 copy-start.4
  341.2 2.9 copy-start.2
  344.1 1.8 copy-start.3
  350.6 1.3 copy-start.4
  361.1 2.9 copy-start.2
  364.1 1.8 copy-start.3
  370.5 1.3 copy-start.4
  381.0 2.9 copy-start.2
  384.0 1.8 copy-start.3
  390.4 1.3 copy-start.4
  400.9 2.9 copy-start.2
  403.9 1.8 copy-start.3
  410.3 1.3 copy-start.4
  420.8 2.9 copy-start.2
  423.8 1.8 copy-start.3
  430.2 1.3 copy-start.4
  440.7 2.9 copy-start.2
  443.7 1.8 copy-start.3
  450.2 1.3 copy-start.4
  460.7 2.9 copy-start.2
  463.6 1.8 copy-start.3
  470.1 1.3 copy-start.4
  480.6 2.9 copy-start.2
  483.5 1.8 copy-start.3
  490.0 1.3 copy-start.4
  500.5 2.9 copy-start.2
  503.4 1.8 copy-start.3
  509.9 1.3 copy-start.4
  520.4 2.9 copy-start.2
  523.3 1.8 copy-start.3
  529.8 1.3 copy-start.4
  540.3 2.9 copy-start.2
  543.2 1.8 copy-start.3
  549.7 1.3 copy-start.4
  560.2 2.9 copy-start.2
  563.1 1.8 copy-start.3
  569.6 1.3 copy-start.4
  572.6 719.6 %copy-start.1 = (bf16[128,900]{0,1:T(8,128)(2,1)S(1)}, bf16[128,900]{0,1:T(8,128)(2,1)}, u32[]{:S(2)}) copy-start(bf16[128,900]{0,1:T(8,128)(2,1)} %param.16) | copy-start | bytes 691204
  572.7 715.8 %all-reduce.18.cloned.1.call-start = ((), (), s32[]{:S(2)}) async-start(), calls=%async_computation.1 | async-start | bytes 2359296 | tf_op jit(solution)/shard_map/psum | solution.py:242
  (30 other events, 27.7 us)
Sparse Core Ops, SparseCore 0:
  572.8 29.1 all-reduce.19
  608.4 222.2 all-reduce.17
